TPU v7x, 32 devices: a whole 2x2x4 slice. The times are simulated.
32 devices in a mesh: subj: 2 (over x), row: 8 (over z, y), col: 2 (over core).
Axes of the slice: x: 2, y: 2, z: 4, core: 2. Of those that a mesh axis runs over, the one named last changes fastest.
Arguments:
- series: float32 [256, 11392], P(('subj', 'row', 'col')), parts along dimension 0, may hold values from -30 to 30
- tap_values: float32 [17], replicated, may hold values from -4 to 4
- tap_count: int32 [1], replicated, may hold values from 4 to 8
- kept_frames: int32 [32], P('subj'), parts along dimension 0, may hold values from 1 to 8, 96 in all
- band_start: int32 [2], P('subj'), parts along dimension 0, may hold values from 0 to 7296
Outputs:
- fisher_band: bfloat16 [8192, 11392], P('subj', ('row', 'col')), parts along dimension 0
There are 2 independent parts, one for each index of `subj`. A program takes and returns all parts, laid end to end along the dimension named above; an argument that names none is the same for every part. Nothing has to cross between parts.
Inputs may be any that keep to these rules, and one draw needn't show every extreme that they name: `tap_count`: frames farther than this from the centre get no weight. Time block d holds frames d * 8 to (d + 1) * 8 - 1; only its first kept_frames[d] frames are kept. `band_start`: the 4096 band grayordinates lie inside the grid.
All inputs are finite; a program needn't handle non-finite values.
Results may differ from a plain program's by a relative error of at most 0.0031.
The roundings to bfloat16 on the way count: a program that leaves them out, or rounds other values in their place, can miss the bound.
Values may be sent and summed in bfloat16 or wider, within the bound.
No kernel may reach another device: no remote copies, remote signals or barrier semaphores. Data moves between devices by JAX's collectives and lax.ppermute only.
A program may use at most 128 MiB of HBM per device.

v0:
```python
import jax
import jax.numpy as jnp
from jax import lax
from jax.sharding import PartitionSpec as P

B = 4096
EPSILON = 1e-06
CLIP_LIMIT = 0.999


def with_halo(cells, sides, width):
    for axis, dim in sides:
        count = lax.axis_size(axis)
        ends = count - 1
        head = lax.slice_in_dim(cells, 0, width, axis=dim)
        tail = lax.slice_in_dim(cells, cells.shape[dim] - width, cells.shape[dim], axis=dim)
        cells = jnp.concatenate(
            [
                lax.ppermute(tail, axis, [(i, (i + 1) % count) for i in range(ends)]),
                cells,
                lax.ppermute(head, axis, [((i + 1) % count, i) for i in range(ends)]),
            ],
            axis=dim,
        )
    return cells


def tap_table(tap_values, tap_count):
    tap_reach = tap_values.shape[0] // 2
    offsets = jnp.arange(tap_values.shape[0], dtype=jnp.int32) - tap_reach
    active = (jnp.abs(offsets) <= tap_count[0]).astype(jnp.float32)
    centre = jnp.sum(active * tap_values) / jnp.sum(active)
    return active * (tap_values - centre)


def band_filter(padded, tap_weights, length):
    filtered = tap_weights[0] * padded[0:length]
    for tap_index in range(1, tap_weights.shape[0]):
        filtered = filtered + tap_weights[tap_index] * padded[tap_index : tap_index + length]
    return filtered


def fisher_z(correlation):
    clipped = jnp.clip(correlation, -CLIP_LIMIT, CLIP_LIMIT)
    return 0.5 * (jnp.log1p(clipped) - jnp.log1p(-clipped))


def body(series, tap_values, tap_count, kept_frames, band_start):
    tap_reach = tap_values.shape[0] // 2
    tap_weights = tap_table(tap_values, tap_count)
    block_len = series.shape[0]
    padded = with_halo(series, ((("row", "col"), 0),), tap_reach)
    filtered = band_filter(padded, tap_weights, block_len)
    own_kept = kept_frames[lax.axis_index(("row", "col"))]
    keep_mask = (jnp.arange(block_len, dtype=jnp.int32) < own_kept).astype(jnp.float32)[:, None]
    centered = keep_mask * filtered
    spread = lax.psum(jnp.sum(centered * centered, axis=0), ("row", "col"))
    scaled = (centered * lax.rsqrt(spread + EPSILON)).astype(jnp.bfloat16)
    columns = lax.all_to_all(scaled, ("row", "col"), split_axis=1, concat_axis=0, tiled=True)
    band_slice = lax.dynamic_slice_in_dim(scaled, band_start[0], B, 1)
    band_cols = lax.all_gather(band_slice, ("row", "col"), axis=0, tiled=True)
    correlation = lax.dot_general(
        band_cols, columns, (((0,), (0,)), ((), ())), preferred_element_type=jnp.float32
    )
    return fisher_z(correlation).astype(jnp.bfloat16)


def solution(mesh):
    placed = (P(("subj", "row", "col"), None), P(), P(), P("subj"), P("subj"))
    return jax.shard_map(
        body, mesh=mesh, in_specs=placed, out_specs=P("subj", ("row", "col")), check_vma=False
    )
```

profile of v0, /device:TPU:0, one launch (start us, length us, event | category | flops | bytes accessed | tf_op | source)
XLA Modules:
  0.0 151.6 jit_solution(5790544908060387476)
XLA Ops:
  6.5 0.0 all-gather.2.cloned.1.call-start
  6.5 2.4 %collective-permute-start = (f32[8,11392]{1,0:T(8,128)}, f32[8,11392]{1,0:T(8,128)S(1)}, u32[]{:S(2)}, u32[]{:S(2)}) collective-permute-start(f32[8,11392]{1,0:T(8,128)} %param.5), channel_id=1, source_target_pairs={{0,1},{1,2},{2,3},{3,4},{4,5},{5,6},{6,7},{7,8},{8,9},{9,10},{10,1... | collective-permute-start | bytes 1093640 | tf_op jit(solution)/shard_map/ppermute | solution.py:19
  8.9 1.3 collective-permute-start.1
  10.9 1.3 dynamic_slice.6
  12.1 1.3 convert_reduce_fusion
  13.5 0.6 compare_convert_fusion
  16.1 0.7 subtract_select_fusion
  16.7 0.7 fusion.19
  17.4 0.0 collective-permute-done
  17.5 1.0 constant_dynamic-update-slice_fusion
  18.5 0.0 collective-permute-done.1
  18.6 12.4 %multiply_reduce_fusion = (f32[11392]{0:T(1024)S(1)}, f32[8,11392]{1,0:T(8,128)S(1)}) fusion(f32[8,11392]{1,0:T(8,128)S(1)} %collective-permute-done.1, f32[]{:T(128)} %bitcast.18, f32[16,11392]{1,0:T(8,128)S(1)} %constant_dynamic-update-slice_fusion.2, f32[]{:T(128)} %bitcast.17, f32[]{:T(128)} %bitcast.16, f32[]{:T(128)} %bitcast.15, f32[]{:T(128)} %bitcast.14, ...), kind=kLoop, calls=%fused_computation.33 | loop fusion | flops 3269504 | bytes 6607460 | tf_op jit(solution)/shard_map/reduce_sum | solution.py:57
  31.0 63.9 %psum.7 = f32[11392]{0:T(1024)S(1)} all-reduce(f32[11392]{0:T(1024)S(1)} %get-tuple-element.5), channel_id=1, replica_groups=mesh['subj'=2,'row'=8,'col'=2] {'row','col'}, use_global_device_ids=true, to_apply=%region_3.0 | all-reduce | flops 11392 | bytes 91136 | tf_op jit(solution)/shard_map/psum | solution.py:57
  94.9 0.7 constant_dynamic-slice_fusion
  95.7 0.0 all-gather.2.cloned.1.call-update
  95.7 0.4 all_to_all.14
  96.1 0.1 copy.6
  96.2 12.3 %all_to_all.19 = bf16[8,16,712]{2,0,1:T(8,128)(2,1)S(1)} all-to-all(bf16[8,16,712]{2,0,1:T(8,128)(2,1)S(1)} %copy.6), channel_id=1, replica_groups=mesh['subj'=2,'row'=8,'col'=2] {'row','col'}, dimensions={1} | all-to-all | bytes 364544 | tf_op jit(solution)/shard_map/all_to_all | solution.py:59
  108.5 23.6 %all-gather.2.cloned.1.call-done = bf16[128,4096]{1,0:T(8,128)(2,1)} async-done(((bf16[8,4096]{1,0:T(8,128)(2,1)}), bf16[128,4096]{1,0:T(8,128)(2,1)}) %all-gather.2.cloned.1.call-update) | async-done | bytes 1048592 | tf_op jit(solution)/shard_map/all_gather | solution.py:61
  132.1 12.7 %multiply_convert_fusion = bf16[4096,712]{0,1:T(8,128)(2,1)} fusion(bf16[128,4096]{1,0:T(8,128)(2,1)} %all-gather.2.cloned.1.call-done, bf16[8,16,712]{2,0,1:T(8,128)(2,1)S(1)} %all_to_all.19), kind=kOutput, calls=%fused_computation | convolution fusion | flops 761167872 | bytes 7063552 | tf_op jit(solution)/shard_map/dot_general | solution.py:62
  (4 shorter events, 0.1 us)
Async XLA Ops:
  6.5 125.6 %all-gather.2.cloned.1.call-start = ((), (), s32[]{:S(2)}) async-start(), calls=%async_computation.1 | async-start | bytes 1114112 | tf_op jit(solution)/shard_map/all_gather | solution.py:61
  6.5 10.9 %collective-permute-start = (f32[8,11392]{1,0:T(8,128)}, f32[8,11392]{1,0:T(8,128)S(1)}, u32[]{:S(2)}, u32[]{:S(2)}) collective-permute-start(f32[8,11392]{1,0:T(8,128)} %param.5), channel_id=1, source_target_pairs={{0,1},{1,2},{2,3},{3,4},{4,5},{5,6},{6,7},{7,8},{8,9},{9,10},{10,1... | collective-permute-start | bytes 1093640 | tf_op jit(solution)/shard_map/ppermute | solution.py:19
  8.9 9.6 %collective-permute-start.1 = (f32[8,11392]{1,0:T(8,128)}, f32[8,11392]{1,0:T(8,128)S(1)}, u32[]{:S(2)}, u32[]{:S(2)}) collective-permute-start(f32[8,11392]{1,0:T(8,128)} %param.5), channel_id=1, source_target_pairs={{1,0},{2,1},{3,2},{4,3},{5,4},{6,5},{7,6},{8,7},{9,8},{10,9},{11,1... | collective-permute-start | bytes 1093640 | tf_op jit(solution)/shard_map/ppermute | solution.py:21
Sparse Core Ops, SparseCore 0:
  95.8 36.2 all-gather.1
where the time goes:
time: 152 us
  blocking collectives  76.2 us (50%)
  waiting for transfers between devices  23.6 us (16%)
  between operations  16.1 us (11%)
  other arithmetic  15.1 us (10%)
  matrix products  12.7 us (8%)
  local copies, waits for them, and re-layouts  4.28 us (3%)
  starting transfers between devices  3.66 us (2%)
    psum x1, blocking collectives, body(): spread = lax.psum(jnp.sum(centered * centered, axis=0), ('row', 'col'))  63.9 us
    all_gather x1, waiting for transfers between devices, body(): band_cols = lax.all_gather(band_slice, ('row', 'col'), axis=0, tiled=True)  23.6 us
    dot_general x1, matrix products, body(): lax.dot_general(band_cols, columns, (((0,), (0,)), ((), ())), preferred_e...  12.7 us
    reduce_sum x1, other arithmetic, body(): spread = lax.psum(jnp.sum(centered * centered, axis=0), ('row', 'col'))  12.4 us
    all_to_all x1, blocking collectives, body(): lax.all_to_all(scaled, ('row', 'col'), split_axis=1, concat_axis=0, tiled...  12.3 us
  transfers between devices with their start and end apart: 3, of which 1 were waited for; matrix products, arithmetic and copies ran while one was open for 4% of the time, Pallas kernels for 0%

commit v1 on v0

--- a/solution.py
+++ b/solution.py
@@ -6,6 +6,28 @@
 B = 4096
 EPSILON = 1e-06
 CLIP_LIMIT = 0.999
+
+
+def in_order(tiles, dim):
+    tiles = jnp.moveaxis(tiles, 0, dim)
+    shape = tiles.shape
+    return tiles.reshape(*shape[:dim], shape[dim] * shape[dim + 1], *shape[dim + 2 :])
+
+
+def collect(value, axis, dim):
+    size = lax.axis_size(axis)
+    pairs = [(i, (i + 1) % size) for i in range(size)]
+    back = [(b, a) for a, b in pairs]
+    lower, upper = ([], [])
+    for step in range(size - 1):
+        if step % 2 == 0:
+            lower.append(lax.ppermute(lower[-1] if lower else value, axis, pairs))
+        else:
+            upper.append(lax.ppermute(upper[-1] if upper else value, axis, back))
+    blocks = jnp.stack([*lower[::-1], value, *upper])
+    shift = lax.axis_index(axis) - len(lower)
+    blocks = blocks[(jnp.arange(size) - shift) % size]
+    return in_order(blocks, dim)
 
 
 def with_halo(cells, sides, width):
@@ -58,7 +80,7 @@
     scaled = (centered * lax.rsqrt(spread + EPSILON)).astype(jnp.bfloat16)
     columns = lax.all_to_all(scaled, ("row", "col"), split_axis=1, concat_axis=0, tiled=True)
     band_slice = lax.dynamic_slice_in_dim(scaled, band_start[0], B, 1)
-    band_cols = lax.all_gather(band_slice, ("row", "col"), axis=0, tiled=True)
+    band_cols = collect(band_slice, ("row", "col"), 0)
     correlation = lax.dot_general(
         band_cols, columns, (((0,), (0,)), ((), ())), preferred_element_type=jnp.float32
     )

time: 152 us -> 161 us (1.059)
  starting transfers between devices: 3.66 us -> 41 us
  between operations: 16.1 us -> 2.85 us
  blocking collectives: 76.2 us -> 63.9 us
  waiting for transfers between devices: 23.6 us -> 21.2 us
    ppermute x0 -> x15, starting transfers between devices: none -> 31.6 us  [the longest x7 31.5 us: collect(): upper.append(lax.ppermute(upper[-1] if upper else value, axis, back))]
    all_gather x1 -> x0, waiting for transfers between devices: 23.6 us -> none  [body(): band_cols = lax.all_gather(band_slice, ('row', 'col'), axis=0, tiled=True)]
    ppermute x0 -> x15, waiting for transfers between devices: none -> 19.4 us  [the longest x8 17.7 us: collect(): lower.append(lax.ppermute(lower[-1] if lower else value, axis, pairs))]
    all_to_all x1 -> x0, blocking collectives: 12.3 us -> none  [body(): lax.all_to_all(scaled, ('row', 'col'), split_axis=1, concat_axis=0, tiled...]
    all_to_all x0 -> x1, starting transfers between devices: none -> 5.82 us  [body(): lax.all_to_all(scaled, ('row', 'col'), split_axis=1, concat_axis=0, tiled...]
    all_to_all x0 -> x1, waiting for transfers between devices: none -> 1.84 us  [body(): lax.all_to_all(scaled, ('row', 'col'), split_axis=1, concat_axis=0, tiled...]
  transfers between devices with their start and end apart: 3 -> 18, of which waited for: 1 -> 9; matrix products, arithmetic and copies ran while one was open for 4% -> 4% of each run, Pallas kernels for 0% -> 0%
where the time goes in v1:
time: 161 us
  blocking collectives  63.9 us (40%)
  starting transfers between devices  41 us (25%)
  waiting for transfers between devices  21.2 us (13%)
  other arithmetic  15 us (9%)
  matrix products  11.5 us (7%)
  local copies, waits for them, and re-layouts  5.1 us (3%)
  between operations  2.85 us (2%)
    psum x1, blocking collectives, body(): spread = lax.psum(jnp.sum(centered * centered, axis=0), ('row', 'col'))  63.9 us
    ppermute x7, starting transfers between devices, collect(): upper.append(lax.ppermute(upper[-1] if upper else value, axis, back))  31.5 us
    ppermute x8, waiting for transfers between devices, collect(): lower.append(lax.ppermute(lower[-1] if lower else value, axis, pairs))  17.7 us
    reduce_sum x1, other arithmetic, body(): spread = lax.psum(jnp.sum(centered * centered, axis=0), ('row', 'col'))  12.4 us
    dot_general x1, matrix products, body(): lax.dot_general(band_cols, columns, (((0,), (0,)), ((), ())), preferred_e...  11.5 us
    all_to_all x1, starting transfers between devices, body(): lax.all_to_all(scaled, ('row', 'col'), split_axis=1, concat_axis=0, tiled...  5.82 us
  transfers between devices with their start and end apart: 18, of which 9 were waited for; matrix products, arithmetic and copies ran while one was open for 4% of the time, Pallas kernels for 0%

profile of v1, /device:TPU:0, one launch (start us, length us, event | category | flops | bytes accessed | tf_op | source)
XLA Modules:
  0.0 160.6 jit_solution(198182982425826788)
XLA Ops:
  0.0 2.4 %collective-permute-start = (f32[8,11392]{1,0:T(8,128)}, f32[8,11392]{1,0:T(8,128)S(1)}, u32[]{:S(2)}, u32[]{:S(2)}) collective-permute-start(f32[8,11392]{1,0:T(8,128)} %param.5), channel_id=1, source_target_pairs={{0,1},{1,2},{2,3},{3,4},{4,5},{5,6},{6,7},{7,8},{8,9},{9,10},{10,1... | collective-permute-start | bytes 1093640 | tf_op jit(solution)/shard_map/ppermute | solution.py:41
  2.4 1.3 collective-permute-start.1
  4.3 1.2 dynamic_slice.6
  5.6 1.3 convert_reduce_fusion
  11.9 12.4 %multiply_reduce_fusion = (f32[11392]{0:T(1024)S(1)}, f32[8,11392]{1,0:T(8,128)S(1)}) fusion(f32[8,11392]{1,0:T(8,128)S(1)} %collective-permute-done.1, f32[]{:T(128)} %bitcast.18, f32[16,11392]{1,0:T(8,128)S(1)} %constant_dynamic-update-slice_fusion.2, f32[]{:T(128)} %bitcast.17, f32[]{:T(128)} %bitcast.16, f32[]{:T(128)} %bitcast.15, f32[]{:T(128)} %bitcast.14, ...), kind=kLoop, calls=%fused_computation.35 | loop fusion | flops 3269504 | bytes 6607460 | tf_op jit(solution)/shard_map/reduce_sum | solution.py:79
  24.3 63.9 %psum.7 = f32[11392]{0:T(1024)S(1)} all-reduce(f32[11392]{0:T(1024)S(1)} %get-tuple-element.5), channel_id=1, replica_groups=mesh['subj'=2,'row'=8,'col'=2] {'row','col'}, use_global_device_ids=true, to_apply=%region_3.0 | all-reduce | flops 11392 | bytes 91136 | tf_op jit(solution)/shard_map/psum | solution.py:79
  88.5 6.4 %collective-permute-done.2 = bf16[8,4096]{1,0:T(8,128)(2,1)S(1)} collective-permute-done((bf16[8,4096]{1,0:T(8,128)(2,1)S(1)}, bf16[8,4096]{1,0:T(8,128)(2,1)S(1)}, u32[]{:S(2)}, u32[]{:S(2)}) %collective-permute-start.2) | collective-permute-done | bytes 65568 | tf_op jit(solution)/shard_map/ppermute | solution.py:24
  94.8 4.4 %collective-permute-start.10 = (bf16[8,4096]{1,0:T(8,128)(2,1)S(1)}, bf16[8,4096]{1,0:T(8,128)(2,1)S(1)}, u32[]{:S(2)}, u32[]{:S(2)}) collective-permute-start(bf16[8,4096]{1,0:T(8,128)(2,1)S(1)} %constant_dynamic-slice_fusion), channel_id=1, source_target_pairs={{1,0},{2,1},{3,2},{4,3},{5,4},{6,5},{7,6},{8,7},{9,8},{10,9},{11,1... | collective-permute-start | bytes 196616 | tf_op jit(solution)/shard_map/ppermute | solution.py:26
  99.3 1.9 %collective-permute-done.3 = bf16[8,4096]{1,0:T(8,128)(2,1)S(1)} collective-permute-done((bf16[8,4096]{1,0:T(8,128)(2,1)S(1)}, bf16[8,4096]{1,0:T(8,128)(2,1)S(1)}, u32[]{:S(2)}, u32[]{:S(2)}) %collective-permute-start.3) | collective-permute-done | bytes 65568 | tf_op jit(solution)/shard_map/ppermute | solution.py:24
  101.2 4.5 %collective-permute-start.11 = (bf16[8,4096]{1,0:T(8,128)(2,1)S(1)}, bf16[8,4096]{1,0:T(8,128)(2,1)S(1)}, u32[]{:S(2)}, u32[]{:S(2)}) collective-permute-start(bf16[8,4096]{1,0:T(8,128)(2,1)S(1)} %collective-permute-done.10), channel_id=1, source_target_pairs={{1,0},{2,1},{3,2},{4,3},{5,4},{6,5},{7,6},{8,7},{9,8},{10,9},{11,1... | collective-permute-start | bytes 196616 | tf_op jit(solution)/shard_map/ppermute | solution.py:26
  105.7 1.9 %collective-permute-done.4 = bf16[8,4096]{1,0:T(8,128)(2,1)S(1)} collective-permute-done((bf16[8,4096]{1,0:T(8,128)(2,1)S(1)}, bf16[8,4096]{1,0:T(8,128)(2,1)S(1)}, u32[]{:S(2)}, u32[]{:S(2)}) %collective-permute-start.4) | collective-permute-done | bytes 65568 | tf_op jit(solution)/shard_map/ppermute | solution.py:24
  107.6 4.5 %collective-permute-start.12 = (bf16[8,4096]{1,0:T(8,128)(2,1)S(1)}, bf16[8,4096]{1,0:T(8,128)(2,1)S(1)}, u32[]{:S(2)}, u32[]{:S(2)}) collective-permute-start(bf16[8,4096]{1,0:T(8,128)(2,1)S(1)} %collective-permute-done.11), channel_id=1, source_target_pairs={{1,0},{2,1},{3,2},{4,3},{5,4},{6,5},{7,6},{8,7},{9,8},{10,9},{11,1... | collective-permute-start | bytes 196616 | tf_op jit(solution)/shard_map/ppermute | solution.py:26
  112.1 1.9 %collective-permute-done.5 = bf16[8,4096]{1,0:T(8,128)(2,1)S(1)} collective-permute-done((bf16[8,4096]{1,0:T(8,128)(2,1)S(1)}, bf16[8,4096]{1,0:T(8,128)(2,1)S(1)}, u32[]{:S(2)}, u32[]{:S(2)}) %collective-permute-start.5) | collective-permute-done | bytes 65568 | tf_op jit(solution)/shard_map/ppermute | solution.py:24
  114.0 4.5 %collective-permute-start.13 = (bf16[8,4096]{1,0:T(8,128)(2,1)S(1)}, bf16[8,4096]{1,0:T(8,128)(2,1)S(1)}, u32[]{:S(2)}, u32[]{:S(2)}) collective-permute-start(bf16[8,4096]{1,0:T(8,128)(2,1)S(1)} %collective-permute-done.12), channel_id=1, source_target_pairs={{1,0},{2,1},{3,2},{4,3},{5,4},{6,5},{7,6},{8,7},{9,8},{10,9},{11,1... | collective-permute-start | bytes 196616 | tf_op jit(solution)/shard_map/ppermute | solution.py:26
  118.5 1.9 %collective-permute-done.6 = bf16[8,4096]{1,0:T(8,128)(2,1)S(1)} collective-permute-done((bf16[8,4096]{1,0:T(8,128)(2,1)S(1)}, bf16[8,4096]{1,0:T(8,128)(2,1)S(1)}, u32[]{:S(2)}, u32[]{:S(2)}) %collective-permute-start.6) | collective-permute-done | bytes 65568 | tf_op jit(solution)/shard_map/ppermute | solution.py:24
  120.4 4.5 %collective-permute-start.14 = (bf16[8,4096]{1,0:T(8,128)(2,1)S(1)}, bf16[8,4096]{1,0:T(8,128)(2,1)S(1)}, u32[]{:S(2)}, u32[]{:S(2)}) collective-permute-start(bf16[8,4096]{1,0:T(8,128)(2,1)S(1)} %collective-permute-done.13), channel_id=1, source_target_pairs={{1,0},{2,1},{3,2},{4,3},{5,4},{6,5},{7,6},{8,7},{9,8},{10,9},{11,1... | collective-permute-start | bytes 196616 | tf_op jit(solution)/shard_map/ppermute | solution.py:26
  124.9 1.9 %collective-permute-done.7 = bf16[8,4096]{1,0:T(8,128)(2,1)S(1)} collective-permute-done((bf16[8,4096]{1,0:T(8,128)(2,1)S(1)}, bf16[8,4096]{1,0:T(8,128)(2,1)S(1)}, u32[]{:S(2)}, u32[]{:S(2)}) %collective-permute-start.7) | collective-permute-done | bytes 65568 | tf_op jit(solution)/shard_map/ppermute | solution.py:24
  126.8 4.5 %collective-permute-start.15 = (bf16[8,4096]{1,0:T(8,128)(2,1)S(1)}, bf16[8,4096]{1,0:T(8,128)(2,1)S(1)}, u32[]{:S(2)}, u32[]{:S(2)}) collective-permute-start(bf16[8,4096]{1,0:T(8,128)(2,1)S(1)} %collective-permute-done.14), channel_id=1, source_target_pairs={{1,0},{2,1},{3,2},{4,3},{5,4},{6,5},{7,6},{8,7},{9,8},{10,9},{11,1... | collective-permute-start | bytes 196616 | tf_op jit(solution)/shard_map/ppermute | solution.py:26
  131.3 1.9 %collective-permute-done.8 = bf16[8,4096]{1,0:T(8,128)(2,1)S(1)} collective-permute-done((bf16[8,4096]{1,0:T(8,128)(2,1)S(1)}, bf16[8,4096]{1,0:T(8,128)(2,1)S(1)}, u32[]{:S(2)}, u32[]{:S(2)}) %collective-permute-start.8) | collective-permute-done | bytes 65568 | tf_op jit(solution)/shard_map/ppermute | solution.py:24
  134.3 5.8 %all-to-all-start = ((bf16[8,16,712]{2,0,1:T(8,128)(2,1)}), bf16[8,16,712]{2,0,1:T(8,128)(2,1)S(1)}, u32[]{:S(2)}, u32[]{:S(2)}) async-start(bf16[8,16,712]{2,0,1:T(8,128)(2,1)} %copy.9), calls=%async_computation | async-start | bytes 393216 | tf_op jit(solution)/shard_map/all_to_all | solution.py:81
  140.2 4.6 %collective-permute-start.16 = (bf16[8,4096]{1,0:T(8,128)(2,1)S(1)}, bf16[8,4096]{1,0:T(8,128)(2,1)S(1)}, u32[]{:S(2)}, u32[]{:S(2)}) collective-permute-start(bf16[8,4096]{1,0:T(8,128)(2,1)S(1)} %collective-permute-done.15), channel_id=1, source_target_pairs={{1,0},{2,1},{3,2},{4,3},{5,4},{6,5},{7,6},{8,7},{9,8},{10,9},{11,1... | collective-permute-start | bytes 196616 | tf_op jit(solution)/shard_map/ppermute | solution.py:26
  145.1 1.6 collective-permute-done.16
  147.3 1.8 %all-to-all-done = bf16[8,16,712]{2,0,1:T(8,128)(2,1)S(1)} async-done(((bf16[8,16,712]{2,0,1:T(8,128)(2,1)}), bf16[8,16,712]{2,0,1:T(8,128)(2,1)S(1)}, u32[]{:S(2)}, u32[]{:S(2)}) %all-to-all-start) | async-done | bytes 182304 | tf_op jit(solution)/shard_map/all_to_all | solution.py:81
  149.2 11.5 %multiply_convert_fusion = bf16[4096,712]{0,1:T(8,128)(2,1)} fusion(bf16[16,8,4096]{2,1,0:T(8,128)(2,1)S(1)} %gather_fusion, bf16[8,16,712]{2,0,1:T(8,128)(2,1)S(1)} %all-to-all-done), kind=kOutput, calls=%fused_computation.2 | convolution fusion | flops 761167872 | bytes 7063552 | tf_op jit(solution)/shard_map/dot_general | solution.py:84
  (47 shorter events, 5.3 us)
Async XLA Ops:
  0.0 10.8 %collective-permute-start = (f32[8,11392]{1,0:T(8,128)}, f32[8,11392]{1,0:T(8,128)S(1)}, u32[]{:S(2)}, u32[]{:S(2)}) collective-permute-start(f32[8,11392]{1,0:T(8,128)} %param.5), channel_id=1, source_target_pairs={{0,1},{1,2},{2,3},{3,4},{4,5},{5,6},{6,7},{7,8},{8,9},{9,10},{10,1... | collective-permute-start | bytes 1093640 | tf_op jit(solution)/shard_map/ppermute | solution.py:41
  2.4 9.5 %collective-permute-start.1 = (f32[8,11392]{1,0:T(8,128)}, f32[8,11392]{1,0:T(8,128)S(1)}, u32[]{:S(2)}, u32[]{:S(2)}) collective-permute-start(f32[8,11392]{1,0:T(8,128)} %param.5), channel_id=1, source_target_pairs={{1,0},{2,1},{3,2},{4,3},{5,4},{6,5},{7,6},{8,7},{9,8},{10,9},{11,1... | collective-permute-start | bytes 1093640 | tf_op jit(solution)/shard_map/ppermute | solution.py:43
  88.4 6.4 %collective-permute-start.2 = (bf16[8,4096]{1,0:T(8,128)(2,1)S(1)}, bf16[8,4096]{1,0:T(8,128)(2,1)S(1)}, u32[]{:S(2)}, u32[]{:S(2)}) collective-permute-start(bf16[8,4096]{1,0:T(8,128)(2,1)S(1)} %constant_dynamic-slice_fusion), channel_id=1, source_target_pairs={{0,1},{1,2},{2,3},{3,4},{4,5},{5,6},{6,7},{7,8},{8,9},{9,10},{10,1... | collective-permute-start | bytes 196616 | tf_op jit(solution)/shard_map/ppermute | solution.py:24
  94.8 6.4 %collective-permute-start.3 = (bf16[8,4096]{1,0:T(8,128)(2,1)S(1)}, bf16[8,4096]{1,0:T(8,128)(2,1)S(1)}, u32[]{:S(2)}, u32[]{:S(2)}) collective-permute-start(bf16[8,4096]{1,0:T(8,128)(2,1)S(1)} %collective-permute-done.2), channel_id=1, source_target_pairs={{0,1},{1,2},{2,3},{3,4},{4,5},{5,6},{6,7},{7,8},{8,9},{9,10},{10,1... | collective-permute-start | bytes 196616 | tf_op jit(solution)/shard_map/ppermute | solution.py:24
  94.8 6.4 %collective-permute-start.10 = (bf16[8,4096]{1,0:T(8,128)(2,1)S(1)}, bf16[8,4096]{1,0:T(8,128)(2,1)S(1)}, u32[]{:S(2)}, u32[]{:S(2)}) collective-permute-start(bf16[8,4096]{1,0:T(8,128)(2,1)S(1)} %constant_dynamic-slice_fusion), channel_id=1, source_target_pairs={{1,0},{2,1},{3,2},{4,3},{5,4},{6,5},{7,6},{8,7},{9,8},{10,9},{11,1... | collective-permute-start | bytes 196616 | tf_op jit(solution)/shard_map/ppermute | solution.py:26
  101.2 6.4 %collective-permute-start.4 = (bf16[8,4096]{1,0:T(8,128)(2,1)S(1)}, bf16[8,4096]{1,0:T(8,128)(2,1)S(1)}, u32[]{:S(2)}, u32[]{:S(2)}) collective-permute-start(bf16[8,4096]{1,0:T(8,128)(2,1)S(1)} %collective-permute-done.3), channel_id=1, source_target_pairs={{0,1},{1,2},{2,3},{3,4},{4,5},{5,6},{6,7},{7,8},{8,9},{9,10},{10,1... | collective-permute-start | bytes 196616 | tf_op jit(solution)/shard_map/ppermute | solution.py:24
  101.2 6.4 %collective-permute-start.11 = (bf16[8,4096]{1,0:T(8,128)(2,1)S(1)}, bf16[8,4096]{1,0:T(8,128)(2,1)S(1)}, u32[]{:S(2)}, u32[]{:S(2)}) collective-permute-start(bf16[8,4096]{1,0:T(8,128)(2,1)S(1)} %collective-permute-done.10), channel_id=1, source_target_pairs={{1,0},{2,1},{3,2},{4,3},{5,4},{6,5},{7,6},{8,7},{9,8},{10,9},{11,1... | collective-permute-start | bytes 196616 | tf_op jit(solution)/shard_map/ppermute | solution.py:26
  107.6 6.4 %collective-permute-start.5 = (bf16[8,4096]{1,0:T(8,128)(2,1)S(1)}, bf16[8,4096]{1,0:T(8,128)(2,1)S(1)}, u32[]{:S(2)}, u32[]{:S(2)}) collective-permute-start(bf16[8,4096]{1,0:T(8,128)(2,1)S(1)} %collective-permute-done.4), channel_id=1, source_target_pairs={{0,1},{1,2},{2,3},{3,4},{4,5},{5,6},{6,7},{7,8},{8,9},{9,10},{10,1... | collective-permute-start | bytes 196616 | tf_op jit(solution)/shard_map/ppermute | solution.py:24
  107.6 6.4 %collective-permute-start.12 = (bf16[8,4096]{1,0:T(8,128)(2,1)S(1)}, bf16[8,4096]{1,0:T(8,128)(2,1)S(1)}, u32[]{:S(2)}, u32[]{:S(2)}) collective-permute-start(bf16[8,4096]{1,0:T(8,128)(2,1)S(1)} %collective-permute-done.11), channel_id=1, source_target_pairs={{1,0},{2,1},{3,2},{4,3},{5,4},{6,5},{7,6},{8,7},{9,8},{10,9},{11,1... | collective-permute-start | bytes 196616 | tf_op jit(solution)/shard_map/ppermute | solution.py:26
  114.0 6.4 %collective-permute-start.6 = (bf16[8,4096]{1,0:T(8,128)(2,1)S(1)}, bf16[8,4096]{1,0:T(8,128)(2,1)S(1)}, u32[]{:S(2)}, u32[]{:S(2)}) collective-permute-start(bf16[8,4096]{1,0:T(8,128)(2,1)S(1)} %collective-permute-done.5), channel_id=1, source_target_pairs={{0,1},{1,2},{2,3},{3,4},{4,5},{5,6},{6,7},{7,8},{8,9},{9,10},{10,1... | collective-permute-start | bytes 196616 | tf_op jit(solution)/shard_map/ppermute | solution.py:24
  114.0 6.4 %collective-permute-start.13 = (bf16[8,4096]{1,0:T(8,128)(2,1)S(1)}, bf16[8,4096]{1,0:T(8,128)(2,1)S(1)}, u32[]{:S(2)}, u32[]{:S(2)}) collective-permute-start(bf16[8,4096]{1,0:T(8,128)(2,1)S(1)} %collective-permute-done.12), channel_id=1, source_target_pairs={{1,0},{2,1},{3,2},{4,3},{5,4},{6,5},{7,6},{8,7},{9,8},{10,9},{11,1... | collective-permute-start | bytes 196616 | tf_op jit(solution)/shard_map/ppermute | solution.py:26
  120.4 6.4 %collective-permute-start.7 = (bf16[8,4096]{1,0:T(8,128)(2,1)S(1)}, bf16[8,4096]{1,0:T(8,128)(2,1)S(1)}, u32[]{:S(2)}, u32[]{:S(2)}) collective-permute-start(bf16[8,4096]{1,0:T(8,128)(2,1)S(1)} %collective-permute-done.6), channel_id=1, source_target_pairs={{0,1},{1,2},{2,3},{3,4},{4,5},{5,6},{6,7},{7,8},{8,9},{9,10},{10,1... | collective-permute-start | bytes 196616 | tf_op jit(solution)/shard_map/ppermute | solution.py:24
  120.4 6.4 %collective-permute-start.14 = (bf16[8,4096]{1,0:T(8,128)(2,1)S(1)}, bf16[8,4096]{1,0:T(8,128)(2,1)S(1)}, u32[]{:S(2)}, u32[]{:S(2)}) collective-permute-start(bf16[8,4096]{1,0:T(8,128)(2,1)S(1)} %collective-permute-done.13), channel_id=1, source_target_pairs={{1,0},{2,1},{3,2},{4,3},{5,4},{6,5},{7,6},{8,7},{9,8},{10,9},{11,1... | collective-permute-start | bytes 196616 | tf_op jit(solution)/shard_map/ppermute | solution.py:26
  126.8 6.4 %collective-permute-start.8 = (bf16[8,4096]{1,0:T(8,128)(2,1)S(1)}, bf16[8,4096]{1,0:T(8,128)(2,1)S(1)}, u32[]{:S(2)}, u32[]{:S(2)}) collective-permute-start(bf16[8,4096]{1,0:T(8,128)(2,1)S(1)} %collective-permute-done.7), channel_id=1, source_target_pairs={{0,1},{1,2},{2,3},{3,4},{4,5},{5,6},{6,7},{7,8},{8,9},{9,10},{10,1... | collective-permute-start | bytes 196616 | tf_op jit(solution)/shard_map/ppermute | solution.py:24
  126.8 13.4 %collective-permute-start.15 = (bf16[8,4096]{1,0:T(8,128)(2,1)S(1)}, bf16[8,4096]{1,0:T(8,128)(2,1)S(1)}, u32[]{:S(2)}, u32[]{:S(2)}) collective-permute-start(bf16[8,4096]{1,0:T(8,128)(2,1)S(1)} %collective-permute-done.14), channel_id=1, source_target_pairs={{1,0},{2,1},{3,2},{4,3},{5,4},{6,5},{7,6},{8,7},{9,8},{10,9},{11,1... | collective-permute-start | bytes 196616 | tf_op jit(solution)/shard_map/ppermute | solution.py:26
  133.2 11.6 %collective-permute-start.9 = (bf16[8,4096]{1,0:T(8,128)(2,1)S(1)}, bf16[8,4096]{1,0:T(8,128)(2,1)S(1)}, u32[]{:S(2)}, u32[]{:S(2)}) collective-permute-start(bf16[8,4096]{1,0:T(8,128)(2,1)S(1)} %collective-permute-done.8), channel_id=1, source_target_pairs={{0,1},{1,2},{2,3},{3,4},{4,5},{5,6},{6,7},{7,8},{8,9},{9,10},{10,1... | collective-permute-start | bytes 196616 | tf_op jit(solution)/shard_map/ppermute | solution.py:24
  134.3 14.8 %all-to-all-start = ((bf16[8,16,712]{2,0,1:T(8,128)(2,1)}), bf16[8,16,712]{2,0,1:T(8,128)(2,1)S(1)}, u32[]{:S(2)}, u32[]{:S(2)}) async-start(bf16[8,16,712]{2,0,1:T(8,128)(2,1)} %copy.9), calls=%async_computation | async-start | bytes 393216 | tf_op jit(solution)/shard_map/all_to_all | solution.py:81
  140.2 6.5 %collective-permute-start.16 = (bf16[8,4096]{1,0:T(8,128)(2,1)S(1)}, bf16[8,4096]{1,0:T(8,128)(2,1)S(1)}, u32[]{:S(2)}, u32[]{:S(2)}) collective-permute-start(bf16[8,4096]{1,0:T(8,128)(2,1)S(1)} %collective-permute-done.15), channel_id=1, source_target_pairs={{1,0},{2,1},{3,2},{4,3},{5,4},{6,5},{7,6},{8,7},{9,8},{10,9},{11,1... | collective-permute-start | bytes 196616 | tf_op jit(solution)/shard_map/ppermute | solution.py:26
